TPU v7x, 32 devices: a whole 2x2x4 slice. The times are simulated.
32 devices in a mesh: seq: 16 (over z, x, core), head: 2 (over y).
Axes of the slice: x: 2, y: 2, z: 4, core: 2. Of those that a mesh axis runs over, the one named last changes fastest.
Arguments:
- byte_rows: bfloat16 [16384, 1024], P('seq', 'head'), may hold values from -6 to 6
- pool_weight: bfloat16 [4, 1024, 1024], P(None, 'head'), may hold values from -0.09375 to 0.09375
- norm_gain: float32 [1024], replicated, may hold values from 0.1 to 1.9
- qkv_weight: bfloat16 [1024, 8, 3, 128], P(None, 'head')
- span_order: int32 [16], replicated, may hold values from 0 to 15, as said below
- query_start: int32 [1], replicated, may hold values from 2560 to 3072
Outputs:
- shortened: bfloat16 [4096, 1024], P('seq', 'head')
- context: bfloat16 [1024, 1024], P('seq', 'head')
- row_highest: float32 [8, 1024], P('head', 'seq')
Inputs may be any that keep to these rules, and one draw needn't show every extreme that they name: `span_order`: entry i is (i + r) mod 16 for one r of each draw.
All inputs are finite; a program needn't handle non-finite values.
Results may differ from a plain program's by a relative error of at most 0.015.
Values may be sent and summed in bfloat16 or wider, within the bound.
A program may use at most 64 MiB of HBM per device.

v0:
```python
import jax
import jax.numpy as jnp
from jax import lax
from jax.sharding import PartitionSpec as P

SF = 4
QROWS_DEV = 64


norm_epsilon = 1e-06
masked_score = -1e30


def extended(block, sides, width):
    for axis, dim in sides:
        count = lax.axis_size(axis)
        forward = [(i, i + 1) for i in range(count - 1)]
        forward.append((count - 1, 0))
        backward = [(target, source) for source, target in forward]
        low = lax.ppermute(
            lax.slice_in_dim(block, block.shape[dim] - width, None, axis=dim), axis, forward
        )
        high = lax.ppermute(lax.slice_in_dim(block, 0, width, axis=dim), axis, backward)
        block = jnp.concatenate([low, block, high], axis=dim)
    return block


def deliver_queries(placed, pair_count):
    slots = placed.reshape(pair_count, QROWS_DEV, placed.shape[1], placed.shape[2]).astype(
        jnp.bfloat16
    )
    received = lax.all_to_all(slots, "seq", split_axis=0, concat_axis=0, tiled=True)
    return jnp.sum(received.astype(jnp.float32), axis=0).astype(jnp.bfloat16)


def body(byte_rows, pool_weight, norm_gain, qkv_weight, span_order, query_start):
    local_rows, features = byte_rows.shape
    half_rows = local_rows // 2
    short_rows = local_rows // SF
    span_rows = short_rows // 2
    model_width = qkv_weight.shape[0]
    heads_here = qkv_weight.shape[1]
    head_width = qkv_weight.shape[3]
    pair_count = lax.axis_size("seq")
    seq_index = lax.axis_index("seq")
    head_index = lax.axis_index("head")
    pair_slots = jnp.arange(pair_count, dtype=jnp.int32)
    my_pair = jnp.sum(jnp.where(pair_slots == seq_index, span_order, 0))
    shift_rows = SF - 1
    first_tail = byte_rows[half_rows - shift_rows : half_rows]
    outgoing = jnp.concatenate([byte_rows[local_rows - shift_rows :], first_tail], axis=0)
    padded = extended(outgoing, (("seq", 0),), shift_rows)
    from_before = padded[:shift_rows]
    from_after = padded[padded.shape[0] - shift_rows :]
    first_prev = jnp.where(my_pair == 0, jnp.zeros_like(from_before), from_before)
    second_prev = jnp.where(my_pair == pair_count - 1, first_tail, from_after)
    grouped = jnp.concatenate(
        [
            first_prev,
            byte_rows[: half_rows - shift_rows],
            second_prev,
            byte_rows[half_rows : local_rows - shift_rows],
        ],
        axis=0,
    )
    grouped = grouped.reshape(short_rows, SF * features)
    partial_value = jnp.dot(
        grouped, pool_weight.reshape(SF * features, model_width), preferred_element_type=jnp.float32
    )
    qkv_flat = qkv_weight.reshape(model_width, heads_here * 3 * head_width)
    shortened = lax.psum_scatter(partial_value, "head", scatter_dimension=1, tiled=True).astype(
        jnp.bfloat16
    )
    widened = shortened.astype(jnp.float32)
    squares = lax.psum(jnp.sum(widened * widened, axis=1, keepdims=True), "head") / model_width
    gain_here = lax.dynamic_slice_in_dim(norm_gain, head_index * features, features, 0)
    normed_part = (widened * lax.rsqrt(squares + norm_epsilon) * gain_here).astype(jnp.bfloat16)
    projected = jnp.dot(
        lax.all_gather(normed_part, "head", axis=1, tiled=True),
        qkv_flat,
        preferred_element_type=jnp.float32,
    )
    projected = projected.astype(jnp.bfloat16).reshape(short_rows, heads_here, 3, head_width)
    own_spans = (my_pair, 2 * pair_count - 1 - my_pair)
    query_total = QROWS_DEV * pair_count
    window_start = query_start[0]
    own_queries = projected[:, :, 0]
    local_index = jnp.arange(span_rows, dtype=jnp.int32)

    def place_half(half_index):
        span_id = own_spans[half_index]
        positions = span_id * span_rows + local_index
        inside = (positions >= window_start) & (positions < window_start + query_total)
        rows_here = own_queries[half_index * span_rows : (half_index + 1) * span_rows].astype(
            jnp.float32
        )
        values_in = jnp.where(inside[:, None, None], rows_here, 0.0)
        at_row = jnp.clip(span_id * span_rows - window_start, -span_rows, query_total) + span_rows
        canvas = jnp.zeros((query_total + 2 * span_rows, heads_here, head_width), jnp.float32)
        return lax.dynamic_update_slice(canvas, values_in, (at_row, jnp.int32(0), jnp.int32(0)))

    placed = (place_half(0) + place_half(1))[span_rows : span_rows + query_total]
    my_queries = deliver_queries(placed, pair_count)
    score_scale = head_width ** (-0.5)

    def piece_positions(count):
        row_numbers = jnp.arange(count, dtype=jnp.int32)
        owner_dev = row_numbers // short_rows
        second = row_numbers // span_rows % 2
        owner_pair = jnp.sum(
            jnp.where(owner_dev[:, None] == pair_slots[None, :], span_order[None, :], 0), axis=1
        )
        span_id = jnp.where(second == 0, owner_pair, 2 * pair_count - 1 - owner_pair)
        return span_id * span_rows + row_numbers % span_rows

    def masked_scores(query_block, query_pos, key_block, key_pos):
        scores = (
            jnp.einsum("qhd,khd->hqk", query_block, key_block, preferred_element_type=jnp.float32)
            * score_scale
        )
        return jnp.where(key_pos[None, None, :] <= query_pos[None, :, None], scores, masked_score)

    query_pos = window_start + seq_index * QROWS_DEV + jnp.arange(QROWS_DEV, dtype=jnp.int32)
    portion = lax.all_gather(projected[:, :, 1], "seq", axis=0, tiled=True)
    scores = masked_scores(my_queries, query_pos, portion, piece_positions(portion.shape[0]))
    highest = jnp.maximum(
        jnp.full((heads_here, QROWS_DEV), masked_score, jnp.float32), jnp.max(scores, axis=2)
    )
    portion = lax.all_gather(projected[:, :, 1:], "seq", axis=0, tiled=True)
    scores = masked_scores(
        my_queries, query_pos, portion[:, :, 0], piece_positions(portion.shape[0])
    )
    weights = jnp.exp(scores - highest[:, :, None]).astype(jnp.bfloat16)
    summed = jnp.einsum(
        "hqk,khd->qhd", weights, portion[:, :, 1], preferred_element_type=jnp.float32
    )
    totals = jnp.sum(weights, axis=2, dtype=jnp.float32)
    summed, totals = (summed, totals)
    context = summed / totals.T[:, :, None]
    row_highest = highest * head_width**0.5
    return (
        shortened,
        context.reshape(QROWS_DEV, heads_here * head_width).astype(jnp.bfloat16),
        row_highest,
    )


def solution(mesh):
    placed = (P("seq", "head"), P(None, "head", None), P(), P(None, "head", None, None), P(), P())
    return jax.shard_map(
        body,
        mesh=mesh,
        in_specs=placed,
        out_specs=(P("seq", "head"), P("seq", "head"), P("head", "seq")),
        check_vma=False,
    )
```

profile of v0, /device:TPU:0, one launch (start us, length us, event | category | flops | bytes accessed | tf_op | source)
XLA Modules:
  0.0 215.5 jit_solution(7884034041708387243)
XLA Ops:
  7.2 0.0 reduce-scatter.2.cloned.1.call-start
  7.2 0.7 slice.41
  7.9 5.4 %collective-permute-start.1 = (bf16[3,512]{1,0:T(4,128)(2,1)S(1)}, bf16[3,512]{1,0:T(4,128)(2,1)S(1)}, u32[]{:S(2)}, u32[]{:S(2)}) collective-permute-start(bf16[3,512]{1,0:T(4,128)(2,1)S(1)} %slice.41), channel_id=1, source_target_pairs={{2,0},{4,2},{6,4},{8,6},{10,8},{12,10},{14,12},{16,14},{18,16},{20... | collective-permute-start | bytes 9224 | tf_op jit(solution)/shard_map/ppermute | solution.py:23
  13.4 1.3 fusion.31
  15.3 0.0 collective-permute-done.1
  15.3 0.7 fusion.32
  16.0 0.0 collective-permute-start
  16.0 1.3 fusion.33
  18.0 3.8 %collective-permute-done = bf16[3,512]{1,0:T(4,128)(2,1)S(1)} collective-permute-done((bf16[3,512]{1,0:T(4,128)(2,1)S(1)}, bf16[3,512]{1,0:T(4,128)(2,1)S(1)}, u32[]{:S(2)}, u32[]{:S(2)}) %collective-permute-start) | collective-permute-done | bytes 3104 | tf_op jit(solution)/shard_map/ppermute | solution.py:20
  21.8 0.3 pad_maximum_fusion
  22.0 1.5 reshape.135
  23.5 0.0 copy-start
  23.5 4.9 %fusion.34 = f32[256,1024]{1,0:T(8,128)} fusion(bf16[256,2048]{1,0:T(8,128)(2,1)} %reshape.135, bf16[2048,1024]{1,0:T(8,128)(2,1)} %bitcast.76), kind=kOutput, calls=%fused_computation.70 | convolution fusion | flops 1073741824 | bytes 6291456 | tf_op jit(solution)/shard_map/dot_general | solution.py:67
  28.4 0.0 copy-start.2
  28.4 0.0 reduce-scatter.2.cloned.1.call-update
  28.4 0.0 all-gather.6.cloned.1.call-start
  28.5 0.0 copy-done
  28.5 4.4 %copy.33 = bf16[1024,4,3,128]{0,3,2,1:T(8,128)(2,1)} copy(bf16[1024,4,3,128]{3,1,2,0:T(4,128)(2,1)S(1)} %copy-done) | data formatting | bytes 6291456 | tf_op args[3]
  32.9 0.0 copy-done.2
  32.9 0.1 dynamic_slice.3
  32.9 13.4 %reduce-scatter.2.cloned.1.call-done = f32[256,512]{1,0:T(8,128)} async-done(((f32[256,1024]{1,0:T(8,128)}), f32[256,512]{1,0:T(8,128)}) %reduce-scatter.2.cloned.1.call-update) | async-done | bytes 524304 | tf_op jit(solution)/shard_map/reduce_scatter | solution.py:71
  46.4 1.2 fusion.14
  47.5 0.0 copy-start.1
  47.5 4.9 %psum.7 = f32[256,1]{0,1:T(1,128)S(1)} all-reduce(f32[256,1]{0,1:T(1,128)S(1)} %bitcast.74), channel_id=1, replica_groups=mesh['seq'=16,'head'=2] {'head'}, use_global_device_ids=true, to_apply=%region_3.4 | all-reduce | flops 256 | bytes 2048 | tf_op jit(solution)/shard_map/psum | solution.py:75
  52.5 0.1 fusion.16
  52.6 7.4 %all_gather.9 = bf16[256,1024]{1,0:T(8,128)(2,1)S(1)} all-gather(bf16[256,512]{1,0:T(8,128)(2,1)S(1)} %fusion.16), channel_id=1, replica_groups=mesh['seq'=16,'head'=2] {'head'}, dimensions={1}, use_global_device_ids=true | all-gather | bytes 786432 | tf_op jit(solution)/shard_map/all_gather | solution.py:79
  60.0 0.0 copy-done.1
  60.0 2.9 %convolution_convert_fusion = bf16[256,1536]{1,0:T(8,128)(2,1)S(1)} fusion(bf16[256,1024]{1,0:T(8,128)(2,1)S(1)} %all_gather.9, bf16[1024,1536]{0,1:T(8,128)(2,1)} %bitcast.72), kind=kOutput, calls=%fused_computation.12 | convolution fusion | flops 805699584 | bytes 4456448 | tf_op jit(solution)/shard_map/dot_general | solution.py:78
  62.9 0.3 copy.34
  63.2 0.8 copy.43
  64.1 0.0 all-gather.6.cloned.1.call-update
  64.1 0.0 all-gather.4.cloned.1.call-start
  64.2 1.0 copy.42
  65.2 0.0 all-gather.4.cloned.1.call-update
  67.2 0.7 convert_select_fusion.1
  67.9 0.2 broadcast.185
  68.1 1.4 dynamic_update_slice.8
  69.6 0.9 fusion.17
  70.4 2.2 %add.128 = f32[1280,4,128]{0,2,1:T(8,128)S(1)} dynamic-update-slice(f32[1280,4,128]{0,2,1:T(8,128)S(1)} %dynamic_update_slice.8, f32[128,4,128]{0,2,1:T(8,128)} %fusion.17, s32[]{:T(128)S(6)} %select_n.109, s32[]{:T(128)} %constant.88.clone.1, s32[]{:T(128)} %constant.88.clone.1) | dynamic-update-slice | bytes 524292 | tf_op jit(solution)/shard_map/add | solution.py:102
  72.6 0.0 copy-start.3
  72.6 1.2 slice.77
  73.9 1.6 copy.37
  75.5 1.1 copy.38
  76.6 5.6 %all-to-all-start = ((bf16[16,64,4,128]{3,1,2,0:T(8,128)(2,1)}), bf16[16,64,4,128]{3,1,2,0:T(8,128)(2,1)S(1)}, u32[]{:S(2)}, u32[]{:S(2)}) async-start(bf16[16,64,4,128]{3,1,2,0:T(8,128)(2,1)} %copy.38), calls=%async_computation.1 | async-start | bytes 2097152 | tf_op jit(solution)/shard_map/all_to_all | solution.py:32
  82.3 0.0 copy-done.3
  82.3 0.1 select_reduce_fusion
  82.4 0.2 broadcast_compare_fusion
  82.6 29.7 %all-to-all-done = bf16[16,64,4,128]{3,1,2,0:T(8,128)(2,1)S(1)} async-done(((bf16[16,64,4,128]{3,1,2,0:T(8,128)(2,1)}), bf16[16,64,4,128]{3,1,2,0:T(8,128)(2,1)S(1)}, u32[]{:S(2)}, u32[]{:S(2)}) %all-to-all-start) | async-done | bytes 1048608 | tf_op jit(solution)/shard_map/all_to_all | solution.py:32
  112.3 0.2 reduce_sum.55
  112.5 14.8 %all-gather.6.cloned.1.call-done = bf16[4096,4,1,128]{3,0,1,2:T(8,128)(2,1)} async-done(((bf16[256,4,1,128]{3,0,1,2:T(8,128)(2,1)}), bf16[4096,4,1,128]{3,0,1,2:T(8,128)(2,1)}) %all-gather.6.cloned.1.call-update) | async-done | bytes 4194320 | tf_op jit(solution)/shard_map/all_gather | solution.py:124
  127.3 3.9 %fusion.7 = f32[4,64]{1,0:T(4,128)S(1)} fusion(bf16[64,4,128]{2,0,1:T(8,128)(2,1)S(1)} %reduce_sum.55, bf16[4096,4,1,128]{3,0,1,2:T(8,128)(2,1)} %all-gather.6.cloned.1.call-done, pred[64,4096]{1,0:T(8,128)(4,1)S(1)} %broadcast_compare_fusion), kind=kOutput, calls=%fused_computation.14 | convolution fusion | flops 271580928 | bytes 4523008 | tf_op jit(solution)/shard_map/qhd,khd->hqk/dot_general | solution.py:118
  131.2 0.6 broadcast_multiply_fusion
  131.7 71.1 %all-gather.4.cloned.1.call-done = bf16[4096,4,2,128]{3,0,1,2:T(8,128)(2,1)} async-done(((bf16[256,4,2,128]{3,0,1,2:T(8,128)(2,1)}), bf16[4096,4,2,128]{3,0,1,2:T(8,128)(2,1)}) %all-gather.4.cloned.1.call-update) | async-done | bytes 8388624 | tf_op jit(solution)/shard_map/all_gather | solution.py:129
  202.9 0.0 copy-start.4
  202.9 4.1 %convert_reduce_fusion = (f32[4,64]{1,0:T(4,128)S(1)}, bf16[4,64,4096]{2,1,0:T(8,128)(2,1)S(1)}) fusion(f32[4,64]{1,0:T(4,128)S(1)} %get-tuple-element.10, bf16[64,4,128]{2,0,1:T(8,128)(2,1)S(1)} %reduce_sum.55, bf16[4096,4,2,128]{3,0,1,2:T(8,128)(2,1)} %all-gather.4.cloned.1.call-done, pred[64,4096]{1,0:T(8,128)(4,1)S(1)} %broadcast_compare_fusion), kind=kOutput, calls=%fused_computation.11 | convolution fusion | flops 274726656 | bytes 6621184 | tf_op jit(solution)/shard_map/qhd,khd->hqk/dot_general | solution.py:118
  207.0 0.5 copy-done.4
  207.5 0.8 fusion.13
  208.4 0.6 copy.46
  (9 shorter events, 0.1 us)
Async XLA Ops:
  7.2 39.2 %reduce-scatter.2.cloned.1.call-start = ((), (), s32[]{:S(2)}) async-start(), calls=%async_computation.2 | async-start | bytes 1572864 | tf_op jit(solution)/shard_map/reduce_scatter | solution.py:71
  7.9 7.4 %collective-permute-start.1 = (bf16[3,512]{1,0:T(4,128)(2,1)S(1)}, bf16[3,512]{1,0:T(4,128)(2,1)S(1)}, u32[]{:S(2)}, u32[]{:S(2)}) collective-permute-start(bf16[3,512]{1,0:T(4,128)(2,1)S(1)} %slice.41), channel_id=1, source_target_pairs={{2,0},{4,2},{6,4},{8,6},{10,8},{12,10},{14,12},{16,14},{18,16},{20... | collective-permute-start | bytes 9224 | tf_op jit(solution)/shard_map/ppermute | solution.py:23
  16.0 5.7 %collective-permute-start = (bf16[3,512]{1,0:T(4,128)(2,1)S(1)}, bf16[3,512]{1,0:T(4,128)(2,1)S(1)}, u32[]{:S(2)}, u32[]{:S(2)}) collective-permute-start(bf16[3,512]{1,0:T(4,128)(2,1)S(1)} %get-tuple-element.5), channel_id=1, source_target_pairs={{0,2},{2,4},{4,6},{6,8},{8,10},{10,12},{12,14},{14,16},{16,18},{18... | collective-permute-start | bytes 9224 | tf_op jit(solution)/shard_map/ppermute | solution.py:20
  23.5 5.0 %copy-start = (bf16[1024,4,3,128]{3,1,2,0:T(4,128)(2,1)S(1)}, bf16[1024,4,3,128]{3,1,2,0:T(4,128)(2,1)}, u32[]{:S(2)}) copy-start(bf16[1024,4,3,128]{3,1,2,0:T(4,128)(2,1)} %param.9) | copy-start | bytes 9437188
  28.4 4.5 %copy-start.2 = (f32[1024]{0:T(1024)S(1)}, f32[1024]{0:T(1024)}, u32[]{:S(2)}) copy-start(f32[1024]{0:T(1024)} %param.8) | copy-start | bytes 12292
  28.4 98.9 %all-gather.6.cloned.1.call-start = ((), (), s32[]{:S(2)}) async-start(), calls=%async_computation.4 | async-start | bytes 4456448 | tf_op jit(solution)/shard_map/all_gather | solution.py:124
  47.5 12.5 %copy-start.1 = (bf16[256,512]{1,0:T(8,128)(2,1)}, bf16[256,512]{1,0:T(8,128)(2,1)S(1)}, u32[]{:S(2)}) copy-start(bf16[256,512]{1,0:T(8,128)(2,1)S(1)} %get-tuple-element.4) | copy-start | bytes 786436
  64.1 138.8 %all-gather.4.cloned.1.call-start = ((), (), s32[]{:S(2)}) async-start(), calls=%async_computation.3 | async-start | bytes 8912896 | tf_op jit(solution)/shard_map/all_gather | solution.py:129
  72.6 9.6 %copy-start.3 = (s32[16]{0:T(128)S(1)}, s32[16]{0:T(128)}, u32[]{:S(2)}) copy-start(s32[16]{0:T(128)} %param.10) | copy-start | bytes 196
  76.6 35.7 %all-to-all-start = ((bf16[16,64,4,128]{3,1,2,0:T(8,128)(2,1)}), bf16[16,64,4,128]{3,1,2,0:T(8,128)(2,1)S(1)}, u32[]{:S(2)}, u32[]{:S(2)}) async-start(bf16[16,64,4,128]{3,1,2,0:T(8,128)(2,1)} %copy.38), calls=%async_computation.1 | async-start | bytes 2097152 | tf_op jit(solution)/shard_map/all_to_all | solution.py:32
  202.9 4.6 %copy-start.4 = (bf16[4096,4,2,128]{3,0,1,2:T(8,128)(2,1)S(1)}, bf16[4096,4,2,128]{3,0,1,2:T(8,128)(2,1)}, u32[]{:S(2)}) copy-start(bf16[4096,4,2,128]{3,0,1,2:T(8,128)(2,1)} %all-gather.4.cloned.1.call-done) | copy-start | bytes 25165828
Sparse Core Ops, SparseCore 0:
  28.5 17.7 reduce-scatter.1
  64.2 63.0 all-gather.5
  129.5 73.3 all-gather.3
where the time goes:
time: 216 us
  waiting for transfers between devices  133 us (62%)
  local copies, waits for them, and re-layouts  19.1 us (9%)
  between operations  17.2 us (8%)
  matrix products  16.6 us (8%)
  blocking collectives  12.3 us (6%)
  starting transfers between devices  11.2 us (5%)
  other arithmetic  6.3 us (3%)
    all_gather x1, waiting for transfers between devices, body(): portion = lax.all_gather(projected[:, :, 1:], 'seq', axis=0, tiled=True)  71.1 us
    all_to_all x1, waiting for transfers between devices, deliver_queries(): lax.all_to_all(slots, 'seq', split_axis=0, concat_axis=0, tiled=True)  29.7 us
    all_gather x1, waiting for transfers between devices, body(): portion = lax.all_gather(projected[:, :, 1], 'seq', axis=0, tiled=True)  14.8 us
    reduce_scatter x1, waiting for transfers between devices, body(): lax.psum_scatter(partial_value, 'head', scatter_dimension=1, tiled=True)  13.4 us
    dot_general x2, matrix products, masked_scores(): jnp.einsum('qhd,khd->hqk', query_block, key_block, preferred_element_type...  7.97 us
    all_gather x1, blocking collectives, body(): lax.all_gather(normed_part, 'head', axis=1, tiled=True)  7.39 us
    unnamed x13, local copies, waits for them, and re-layouts  6.77 us
    all_to_all x1, starting transfers between devices, deliver_queries(): lax.all_to_all(slots, 'seq', split_axis=0, concat_axis=0, tiled=True)  5.61 us
  transfers between devices with their start and end apart: 6, of which 5 were waited for; matrix products, arithmetic and copies ran while one was open for 10% of the time, Pallas kernels for 0%

commit v1 on v0

v1 whole, which is shorter than its diff:
```python
import jax
import jax.numpy as jnp
import functools
from jax import lax
from jax.experimental import pallas as pl
from jax.experimental.pallas import tpu as pltpu
from jax.sharding import PartitionSpec as P

SF = 4
QROWS_DEV = 64


norm_epsilon = 1e-06
masked_score = -1e30


def extended(block, sides, width):
    for axis, dim in sides:
        count = lax.axis_size(axis)
        forward = [(i, i + 1) for i in range(count - 1)]
        forward.append((count - 1, 0))
        backward = [(target, source) for source, target in forward]
        low = lax.ppermute(
            lax.slice_in_dim(block, block.shape[dim] - width, None, axis=dim), axis, forward
        )
        high = lax.ppermute(lax.slice_in_dim(block, 0, width, axis=dim), axis, backward)
        block = jnp.concatenate([low, block, high], axis=dim)
    return block


def attend_kernel(place_ref, q_ref, k_ref, v_ref, o_ref, m_ref, l_ref, *, scale, span_rows):
    first_pos, second_pos, window_start = place_ref[0], place_ref[1], place_ref[2]
    keys, queries = k_ref.shape[0], q_ref.shape[0]
    scores = lax.dot_general(
        k_ref[...], q_ref[...], (((1,), (1,)), ((), ())), preferred_element_type=jnp.float32
    ) * scale
    row = lax.broadcasted_iota(jnp.int32, (keys, 1), 0)
    key_pos = jnp.where(row < span_rows, first_pos + row, second_pos + row - span_rows)
    query_pos = window_start + lax.broadcasted_iota(jnp.int32, (1, queries), 1)
    scores = jnp.where(key_pos <= query_pos, scores, masked_score)
    highest = jnp.max(scores, axis=0, keepdims=True)
    weights = jnp.exp(scores - highest).astype(jnp.bfloat16)
    m_ref[...] = highest[None]
    l_ref[...] = jnp.sum(weights.astype(jnp.float32), axis=0, keepdims=True)[None]
    o_ref[...] = lax.dot_general(
        weights, v_ref[...], (((0,), (0,)), ((), ())), preferred_element_type=jnp.float32
    ).astype(o_ref.dtype)


def attend_local(place, queries, projected, heads, head_width, span_rows):
    count, keys = queries.shape[0], projected.shape[0]
    stat = jax.ShapeDtypeStruct((heads, 1, count), jnp.float32)
    stat_spec = pl.BlockSpec((1, 1, count), lambda h, place: (h, 0, 0))
    return pl.pallas_call(
        functools.partial(attend_kernel, scale=head_width ** (-0.5), span_rows=span_rows),
        grid_spec=pltpu.PrefetchScalarGridSpec(
            num_scalar_prefetch=1,
            grid=(heads,),
            in_specs=[
                pl.BlockSpec((count, head_width), lambda h, place: (0, h)),
                pl.BlockSpec((keys, head_width), lambda h, place: (0, h * 3 + 1)),
                pl.BlockSpec((keys, head_width), lambda h, place: (0, h * 3 + 2)),
            ],
            out_specs=[
                pl.BlockSpec((count, head_width), lambda h, place: (0, h)),
                stat_spec,
                stat_spec,
            ],
        ),
        out_shape=[jax.ShapeDtypeStruct((count, heads * head_width), jnp.bfloat16), stat, stat],
    )(place, queries, projected, projected)


def gather_queries(own):
    return lax.all_gather(own, "seq", axis=0, tiled=False)


def exchange(parts, stats):
    parts = lax.all_to_all(parts, "seq", split_axis=0, concat_axis=0, tiled=True)
    stats = lax.all_to_all(stats, "seq", split_axis=0, concat_axis=0, tiled=True)
    return parts, stats


def body(byte_rows, pool_weight, norm_gain, qkv_weight, span_order, query_start):
    local_rows, features = byte_rows.shape
    half_rows = local_rows // 2
    short_rows = local_rows // SF
    span_rows = short_rows // 2
    model_width = qkv_weight.shape[0]
    heads_here = qkv_weight.shape[1]
    head_width = qkv_weight.shape[3]
    pair_count = lax.axis_size("seq")
    seq_index = lax.axis_index("seq")
    head_index = lax.axis_index("head")
    pair_slots = jnp.arange(pair_count, dtype=jnp.int32)
    my_pair = jnp.sum(jnp.where(pair_slots == seq_index, span_order, 0))
    shift_rows = SF - 1
    first_tail = byte_rows[half_rows - shift_rows : half_rows]
    outgoing = jnp.concatenate([byte_rows[local_rows - shift_rows :], first_tail], axis=0)
    padded = extended(outgoing, (("seq", 0),), shift_rows)
    from_before = padded[:shift_rows]
    from_after = padded[padded.shape[0] - shift_rows :]
    first_prev = jnp.where(my_pair == 0, jnp.zeros_like(from_before), from_before)
    second_prev = jnp.where(my_pair == pair_count - 1, first_tail, from_after)
    grouped = jnp.concatenate(
        [
            first_prev,
            byte_rows[: half_rows - shift_rows],
            second_prev,
            byte_rows[half_rows : local_rows - shift_rows],
        ],
        axis=0,
    )
    grouped = grouped.reshape(short_rows, SF * features)
    partial_value = jnp.dot(
        grouped, pool_weight.reshape(SF * features, model_width), preferred_element_type=jnp.float32
    )
    qkv_flat = qkv_weight.reshape(model_width, heads_here * 3 * head_width)
    if lax.axis_size("head") == 2:
        other = lax.ppermute(partial_value.astype(jnp.bfloat16), "head", [(0, 1), (1, 0)])
        pooled = (partial_value + other.astype(jnp.float32)).astype(jnp.bfloat16)
    else:
        pooled = lax.psum(partial_value, "head").astype(jnp.bfloat16)
    shortened = lax.dynamic_slice_in_dim(pooled, head_index * features, features, 1)
    widened = pooled.astype(jnp.float32)
    squares = jnp.sum(widened * widened, axis=1, keepdims=True) / model_width
    normed = (widened * lax.rsqrt(squares + norm_epsilon) * norm_gain).astype(jnp.bfloat16)
    projected = jnp.dot(normed, qkv_flat, preferred_element_type=jnp.float32).astype(jnp.bfloat16)
    query_total = QROWS_DEV * pair_count
    window_start = query_start[0]
    own_queries = projected[span_rows:].reshape(span_rows, heads_here, 3, head_width)[:, :, 0]
    own_queries = own_queries.reshape(span_rows, heads_here * head_width)
    gathered = gather_queries(own_queries)[::-1].reshape(-1, heads_here * head_width)
    start = span_order[0] * span_rows + window_start - pair_count * span_rows
    queries = lax.dynamic_slice_in_dim(
        jnp.concatenate([gathered, gathered], axis=0), start, query_total, 0
    )
    place = jnp.stack(
        [my_pair * span_rows, (2 * pair_count - 1 - my_pair) * span_rows, window_start]
    ).astype(jnp.int32)
    parts, highest, totals = attend_local(
        place, queries, projected, heads_here, head_width, span_rows
    )
    stats = jnp.stack([highest[:, 0], totals[:, 0]]).reshape(
        2 * heads_here, pair_count, QROWS_DEV
    )
    parts, stats = exchange(
        parts.reshape(pair_count, QROWS_DEV, heads_here * head_width), stats.transpose(1, 0, 2)
    )
    highs, sums = stats[:, :heads_here], stats[:, heads_here:]
    top = jnp.max(highs, axis=0)
    factor = jnp.exp(highs - top)
    total = jnp.sum(factor * sums, axis=0)
    share = (factor / total).transpose(0, 2, 1)
    context = jnp.concatenate(
        [
            jnp.sum(
                parts[:, :, h * head_width : (h + 1) * head_width].astype(jnp.float32)
                * share[:, :, h : h + 1],
                axis=0,
            )
            for h in range(heads_here)
        ],
        axis=1,
    )
    return shortened, context.astype(jnp.bfloat16), top * head_width**0.5


def solution(mesh):
    placed = (P("seq", "head"), P(None, "head", None), P(), P(None, "head", None, None), P(), P())
    return jax.shard_map(
        body,
        mesh=mesh,
        in_specs=placed,
        out_specs=(P("seq", "head"), P("seq", "head"), P("head", "seq")),
        check_vma=False,
    )
```

time: 216 us -> 146 us (0.68)
  waiting for transfers between devices: 133 us -> 68.9 us
  matrix products: 16.6 us -> 7.99 us
  local copies, waits for them, and re-layouts: 19.1 us -> 12.2 us
  Pallas kernels: 0 us -> 5.95 us
  other arithmetic: 6.3 us -> 11 us
  blocking collectives: 12.3 us -> 9.87 us
    all_gather x2 -> x1, waiting for transfers between devices: 85.9 us -> 41.3 us  [gather_queries(): return lax.all_gather(own, 'seq', axis=0, tiled=False)]
    reduce_scatter x1 -> x0, waiting for transfers between devices: 13.4 us -> none  [body(): lax.psum_scatter(partial_value, 'head', scatter_dimension=1, tiled=True)]
    all_to_all x0 -> x1, blocking collectives: none -> 9.87 us  [exchange(): lax.all_to_all(stats, 'seq', split_axis=0, concat_axis=0, tiled=True)]
    all_to_all x1, waiting for transfers between devices: 29.7 us -> 20.1 us  [exchange(): lax.all_to_all(parts, 'seq', split_axis=0, concat_axis=0, tiled=True)]
    dot_general x4 -> x1, matrix products: 11.7 us -> 2.95 us  [body(): jnp.dot(normed, qkv_flat, preferred_element_type=jnp.float32)]
    all_gather x1 -> x0, blocking collectives: 7.39 us -> none  [body(): lax.all_gather(normed_part, 'head', axis=1, tiled=True)]
    pallas_call x0 -> x1, Pallas kernels: none -> 5.95 us  [attend_local(): pl.pallas_call(functools.partial(attend_kernel, scale=head_width ** (-0.5...]
    psum x1 -> x0, blocking collectives: 4.93 us -> none  [body(): lax.psum(jnp.sum(widened * widened, axis=1, keepdims=True), 'head')]
  transfers between devices with their start and end apart: 6 -> 5, of which waited for: 5 -> 4; matrix products, arithmetic and copies ran while one was open for 10% -> 7% of each run, Pallas kernels for 0% -> 0%
where the time goes in v1:
time: 146 us; the launch traced here: 144 us
  waiting for transfers between devices  68.9 us (47%)
  between operations  17.5 us (12%)
  local copies, waits for them, and re-layouts  12.2 us (8%)
  other arithmetic  11 us (8%)
  starting transfers between devices  10.7 us (7%)
  blocking collectives  9.87 us (7%)
  matrix products  7.99 us (5%)
  Pallas kernels  5.95 us (4%)
    all_gather x1, waiting for transfers between devices, gather_queries(): return lax.all_gather(own, 'seq', axis=0, tiled=False)  41.3 us
    all_to_all x1, waiting for transfers between devices, exchange(): lax.all_to_all(parts, 'seq', split_axis=0, concat_axis=0, tiled=True)  20.1 us
    all_to_all x1, blocking collectives, exchange(): lax.all_to_all(stats, 'seq', split_axis=0, concat_axis=0, tiled=True)  9.87 us
    pallas_call x1, Pallas kernels, attend_local(): pl.pallas_call(functools.partial(attend_kernel, scale=head_width ** (-0.5...  5.95 us
    ppermute x1, starting transfers between devices, extended(): lax.ppermute(lax.slice_in_dim(block, 0, width, axis=dim), axis, backward)  5.44 us
    dot_general x1, matrix products, body(): jnp.dot(grouped, pool_weight.reshape(SF * features, model_width), preferr...  5.04 us
    unnamed x11, local copies, waits for them, and re-layouts  4.58 us
    ppermute x1, waiting for transfers between devices, extended(): lax.ppermute(lax.slice_in_dim(block, block.shape[dim] - width, None, axis...  3.8 us
  transfers between devices with their start and end apart: 5, of which 4 were waited for; matrix products, arithmetic and copies ran while one was open for 7% of the time, Pallas kernels for 0%

profile of v1, /device:TPU:0, one launch (start us, length us, event | category | flops | bytes accessed | tf_op | source)
XLA Modules:
  0.0 144.1 jit_solution(16773401187795943807)
XLA Ops:
  7.2 0.0 all-gather.2.cloned.1.call-start
  7.2 0.7 slice.53
  7.9 5.4 %collective-permute-start.1 = (bf16[3,512]{1,0:T(4,128)(2,1)S(1)}, bf16[3,512]{1,0:T(4,128)(2,1)S(1)}, u32[]{:S(2)}, u32[]{:S(2)}) collective-permute-start(bf16[3,512]{1,0:T(4,128)(2,1)S(1)} %slice.53), channel_id=1, source_target_pairs={{2,0},{4,2},{6,4},{8,6},{10,8},{12,10},{14,12},{16,14},{18,16},{20... | collective-permute-start | bytes 9224 | tf_op jit(solution)/shard_map/ppermute | solution.py:26
  13.4 1.3 fusion.8
  15.3 0.0 collective-permute-done.1
  15.3 0.7 fusion.9
  16.0 0.0 collective-permute-start
  16.0 1.3 fusion.10
  18.0 3.8 %collective-permute-done = bf16[3,512]{1,0:T(4,128)(2,1)S(1)} collective-permute-done((bf16[3,512]{1,0:T(4,128)(2,1)S(1)}, bf16[3,512]{1,0:T(4,128)(2,1)S(1)}, u32[]{:S(2)}, u32[]{:S(2)}) %collective-permute-start) | collective-permute-done | bytes 3104 | tf_op jit(solution)/shard_map/ppermute | solution.py:23
  21.8 0.3 pad_maximum_fusion
  22.0 1.5 %reshape.45 = bf16[256,2048]{1,0:T(8,128)(2,1)} reshape(bf16[1024,512]{1,0:T(8,128)(2,1)S(1)} %pad_maximum_fusion) | data formatting | bytes 2097152 | tf_op jit(solution)/shard_map/reshape | solution.py:114
  23.5 0.0 copy-start.1
  23.5 5.0 %fusion.12 = (bf16[256,1024]{1,0:T(8,128)(2,1)}, f32[256,1024]{1,0:T(8,128)}) fusion(bf16[256,2048]{1,0:T(8,128)(2,1)} %reshape.45, bf16[2048,1024]{1,0:T(8,128)(2,1)} %bitcast.35), kind=kOutput, calls=%fused_computation.35 | convolution fusion | flops 1074003968 | bytes 6815744 | tf_op jit(solution)/shard_map/dot_general | solution.py:115
  28.5 1.5 %collective-permute-start.2 = (bf16[256,1024]{1,0:T(8,128)(2,1)}, bf16[256,1024]{1,0:T(8,128)(2,1)}, u32[]{:S(2)}, u32[]{:S(2)}) collective-permute-start(bf16[256,1024]{1,0:T(8,128)(2,1)} %get-tuple-element.23), channel_id=1, source_target_pairs={{0,1},{1,0},{2,3},{3,2},{4,5},{5,4},{6,7},{7,6},{8,9},{9,8},{10,11... | collective-permute-start | bytes 1572872 | tf_op jit(solution)/shard_map/ppermute | solution.py:120
  30.1 0.0 copy-done.1
  30.1 4.4 %copy.13 = bf16[1024,4,3,128]{0,3,2,1:T(8,128)(2,1)} copy(bf16[1024,4,3,128]{3,1,2,0:T(4,128)(2,1)S(1)} %copy-done.1) | data formatting | bytes 6291456 | tf_op args[3]
  34.4 0.0 copy-start.2
  34.4 3.7 %collective-permute-done.2 = bf16[256,1024]{1,0:T(8,128)(2,1)} collective-permute-done((bf16[256,1024]{1,0:T(8,128)(2,1)}, bf16[256,1024]{1,0:T(8,128)(2,1)}, u32[]{:S(2)}, u32[]{:S(2)}) %collective-permute-start.2) | collective-permute-done | bytes 524320 | tf_op jit(solution)/shard_map/ppermute | solution.py:120
  38.1 1.6 %fusion = (f32[256]{0:T(256)S(1)}, bf16[256,1024]{1,0:T(8,128)(2,1)S(1)}) fusion(f32[256,1024]{1,0:T(8,128)} %get-tuple-element.24, bf16[256,1024]{1,0:T(8,128)(2,1)} %collective-permute-done.2), kind=kLoop, calls=%fused_computation.5 | loop fusion | flops 1572608 | bytes 2098176 | tf_op jit(solution)/shard_map/reduce_sum | solution.py:126
  39.7 0.0 copy-done.2
  39.7 3.0 %convolution_convert_fusion.k_ref.v_ref = bf16[256,1536]{1,0:T(8,128)(2,1)S(1)} fusion(bf16[1024,1536]{0,1:T(8,128)(2,1)} %bitcast.24, bf16[256,1024]{1,0:T(8,128)(2,1)S(1)} %get-tuple-element.14, f32[1024]{0:T(1024)S(1)} %copy-done.2, f32[256]{0:T(256)S(1)} %add_rsqrt_fusion), kind=kOutput, calls=%fused_computation.2 | convolution fusion | flops 806748160 | bytes 4461568 | tf_op jit(solution)/shard_map/dot_general | solution.py:128
  42.7 0.0 copy-start
  42.7 0.0 copy-start.3
  42.7 0.2 copy.14
  43.0 0.8 copy.15
  43.8 0.0 all-gather.2.cloned.1.call-update
  45.7 0.0 copy-done.3
  45.8 0.7 pad_add_fusion.place_ref
  46.4 41.3 %all-gather.2.cloned.1.call-done = bf16[16,128,512]{2,1,0:T(8,128)(2,1)} async-done(((bf16[1,128,512]{2,1,0:T(8,128)(2,1)}), bf16[16,128,512]{2,1,0:T(8,128)(2,1)}) %all-gather.2.cloned.1.call-update) | async-done | bytes 2097168 | tf_op jit(solution)/shard_map/all_gather | solution.py:75
  87.7 1.8 %rev.3 = bf16[16,128,512]{2,1,0:T(8,128)(2,1)S(1)} reverse(bf16[16,128,512]{2,1,0:T(8,128)(2,1)} %all-gather.2.cloned.1.call-done), dimensions={0} | reverse | bytes 4194304 | tf_op jit(solution)/shard_map/rev | solution.py:133
  89.5 0.0 copy-done
  89.5 3.0 %fusion.3.q_ref = bf16[1024,512]{1,0:T(8,128)(2,1)} fusion(s32[]{:T(128)S(6)} %select_n.30, bf16[2048,512]{1,0:T(8,128)(2,1)S(1)} %bitcast.23), kind=kLoop, calls=%fused_computation.8 | loop fusion | flops 2097152 | bytes 3145732 | tf_op jit(solution)/shard_map/concatenate | solution.py:136
  92.5 6.0 %shard_map.85 = (bf16[1024,512]{1,0:T(8,128)(2,1)}, f32[4,1,1024]{2,1,0:T(1,128)}, f32[4,1,1024]{2,1,0:T(1,128)}) custom-call(s32[3]{0:T(128)} %pad_add_fusion.place_ref, bf16[1024,512]{1,0:T(8,128)(2,1)} %fusion.3.q_ref, bf16[256,1536]{1,0:T(8,128)(2,1)} %copy-done, bf16[256,1536]{1,0:T(8,128)(2,1)} %copy-done), custom_call_target="tpu_custom_call" | custom-call | tf_op jit(solution)/shard_map/pallas_call | solution.py:54
  98.5 0.8 pad_maximum_fusion.2
  99.3 0.1 reshape.51
  99.4 0.1 reshape.52
  99.5 9.9 %all_to_all.10 = f32[16,1,512]{2,1,0:T(1,128)S(1)} all-to-all(f32[16,1,512]{2,1,0:T(1,128)S(1)} %reshape.52), channel_id=1, replica_groups=mesh['seq'=16,'head'=2] {'seq'}, dimensions={0} | all-to-all | bytes 65536 | tf_op jit(solution)/shard_map/all_to_all | solution.py:80
  109.4 3.7 %all-to-all-start = ((bf16[16,64,512]{2,1,0:T(8,128)(2,1)}), bf16[16,64,512]{2,1,0:T(8,128)(2,1)S(1)}, u32[]{:S(2)}, u32[]{:S(2)}) async-start(bf16[16,64,512]{2,1,0:T(8,128)(2,1)} %bitcast.25), calls=%async_computation | async-start | bytes 2097152 | tf_op jit(solution)/shard_map/all_to_all | solution.py:79
  113.0 0.7 constant_dynamic-slice_fusion
  113.8 0.5 broadcast.14
  114.3 0.7 reduce
  115.0 0.1 reshape.53
  115.1 0.6 broadcast_multiply_fusion
  115.8 20.1 %all-to-all-done = bf16[16,64,512]{2,1,0:T(8,128)(2,1)S(1)} async-done(((bf16[16,64,512]{2,1,0:T(8,128)(2,1)}), bf16[16,64,512]{2,1,0:T(8,128)(2,1)S(1)}, u32[]{:S(2)}, u32[]{:S(2)}) %all-to-all-start) | async-done | bytes 1048608 | tf_op jit(solution)/shard_map/all_to_all | solution.py:79
  135.9 0.7 multiply_reduce_fusion.3
  136.6 0.6 pad_maximum_fusion.1
  (10 shorter events, 0.2 us)
Async XLA Ops:
  7.2 80.6 %all-gather.2.cloned.1.call-start = ((), (), s32[]{:S(2)}) async-start(), calls=%async_computation.2 | async-start | bytes 2228224 | tf_op jit(solution)/shard_map/all_gather | solution.py:75
  7.9 7.4 %collective-permute-start.1 = (bf16[3,512]{1,0:T(4,128)(2,1)S(1)}, bf16[3,512]{1,0:T(4,128)(2,1)S(1)}, u32[]{:S(2)}, u32[]{:S(2)}) collective-permute-start(bf16[3,512]{1,0:T(4,128)(2,1)S(1)} %slice.53), channel_id=1, source_target_pairs={{2,0},{4,2},{6,4},{8,6},{10,8},{12,10},{14,12},{16,14},{18,16},{20... | collective-permute-start | bytes 9224 | tf_op jit(solution)/shard_map/ppermute | solution.py:26
  16.0 5.7 %collective-permute-start = (bf16[3,512]{1,0:T(4,128)(2,1)S(1)}, bf16[3,512]{1,0:T(4,128)(2,1)S(1)}, u32[]{:S(2)}, u32[]{:S(2)}) collective-permute-start(bf16[3,512]{1,0:T(4,128)(2,1)S(1)} %get-tuple-element.15), channel_id=1, source_target_pairs={{0,2},{2,4},{4,6},{6,8},{8,10},{10,12},{12,14},{14,16},{16,18},{18... | collective-permute-start | bytes 9224 | tf_op jit(solution)/shard_map/ppermute | solution.py:23
  23.5 6.6 %copy-start.1 = (bf16[1024,4,3,128]{3,1,2,0:T(4,128)(2,1)S(1)}, bf16[1024,4,3,128]{3,1,2,0:T(4,128)(2,1)}, u32[]{:S(2)}) copy-start(bf16[1024,4,3,128]{3,1,2,0:T(4,128)(2,1)} %param.9) | copy-start | bytes 9437188
  28.5 9.6 %collective-permute-start.2 = (bf16[256,1024]{1,0:T(8,128)(2,1)}, bf16[256,1024]{1,0:T(8,128)(2,1)}, u32[]{:S(2)}, u32[]{:S(2)}) collective-permute-start(bf16[256,1024]{1,0:T(8,128)(2,1)} %get-tuple-element.23), channel_id=1, source_target_pairs={{0,1},{1,0},{2,3},{3,2},{4,5},{5,4},{6,7},{7,6},{8,9},{9,8},{10,11... | collective-permute-start | bytes 1572872 | tf_op jit(solution)/shard_map/ppermute | solution.py:120
  34.4 5.3 %copy-start.2 = (f32[1024]{0:T(1024)S(1)}, f32[1024]{0:T(1024)}, u32[]{:S(2)}) copy-start(f32[1024]{0:T(1024)} %param.8) | copy-start | bytes 12292
  42.7 46.8 %copy-start = (bf16[256,1536]{1,0:T(8,128)(2,1)}, bf16[256,1536]{1,0:T(8,128)(2,1)S(1)}, u32[]{:S(2)}) copy-start(bf16[256,1536]{1,0:T(8,128)(2,1)S(1)} %convolution_convert_fusion.k_ref.v_ref) | copy-start | bytes 2359300
  42.7 3.0 %copy-start.3 = (s32[16]{0:T(128)S(1)}, s32[16]{0:T(128)}, u32[]{:S(2)}) copy-start(s32[16]{0:T(128)} %param.10) | copy-start | bytes 196
  109.4 26.5 %all-to-all-start = ((bf16[16,64,512]{2,1,0:T(8,128)(2,1)}), bf16[16,64,512]{2,1,0:T(8,128)(2,1)S(1)}, u32[]{:S(2)}, u32[]{:S(2)}) async-start(bf16[16,64,512]{2,1,0:T(8,128)(2,1)} %bitcast.25), calls=%async_computation | async-start | bytes 2097152 | tf_op jit(solution)/shard_map/all_to_all | solution.py:79
Sparse Core Ops, SparseCore 0:
  43.9 43.7 all-gather.1
